TPU v7x, 32 devices: a whole 2x2x4 slice. The times are simulated.
32 devices in a mesh: pipe: 4 (over y, core), expert: 4 (over z), dp: 2 (over x).
Axes of the slice: x: 2, y: 2, z: 4, core: 2. Of those that a mesh axis runs over, the one named last changes fastest.
Arguments:
- acts: bfloat16 [256, 3584], P(('pipe', 'expert', 'dp')), may hold values from -6 to 6
- cotangent: bfloat16 [256, 3584], P(('pipe', 'expert', 'dp')), may hold values from -6 to 6
- routes: int32 [256, 1], P(('pipe', 'expert', 'dp')), may hold values from 0 to 1; in each aligned block of 8 rows (0 to 7, 8 to 15, ...) at most 6 rows name the same one
- probs: bfloat16 [256, 1], P(('pipe', 'expert', 'dp')), may hold values from 0.19921875 to 1
- keep: int32 [4, 8], P('pipe', ('expert', 'dp')), may hold values 0 or 1
- w_gate: bfloat16 [4, 4, 3584, 512], P('pipe', 'expert', None, 'dp'), may hold values from -0.09375 to 0.09375
- w_up: bfloat16 [4, 4, 3584, 512], P('pipe', 'expert', None, 'dp'), may hold values from -0.09375 to 0.09375
- w_down: bfloat16 [4, 4, 512, 3584], P('pipe', 'expert', 'dp'), may hold values from -0.1875 to 0.1875
Outputs:
- layer_out: bfloat16 [256, 3584], P(('pipe', 'expert', 'dp'))
- grad_below: bfloat16 [256, 3584], P(('pipe', 'expert', 'dp'))
Inputs may be any that keep to these rules, and one draw needn't show every extreme that they name: `routes`: the 1 expert of a token differ. Among the rows of one device no expert is named more than 6 times, and in every draw some device names some expert exactly 6 times.
All inputs are finite; a program needn't handle non-finite values. No bound on the sum of `keep` on one device may be relied on, other than what follows from the above.
Results may differ from a plain program's by a relative error of at most 0.0075.
Values may be sent and summed in bfloat16 or wider, within the bound.
No kernel may reach another device: no remote copies, remote signals or barrier semaphores. Data moves between devices by JAX's collectives and lax.ppermute only.
A program may use at most 64 MiB of HBM per device.

v0:
```python
import jax
import jax.numpy as jnp
from jax import lax
from jax.sharding import PartitionSpec as P


def from_behind(shard, axis, by):
    count = lax.axis_size(axis)
    pairs = [(i, i + by) for i in range(count) if 0 <= i + by < count]
    return lax.ppermute(shard, axis, pairs)


def expert_pass(input_rows, rows_cot, gate_cols, up_cols, down_rows):
    contract = (((1,), (1,)), ((), ()))
    gate_pre = jnp.dot(input_rows, gate_cols, preferred_element_type=jnp.float32)
    up_pre = jnp.dot(input_rows, up_cols, preferred_element_type=jnp.float32)
    squash = jax.nn.sigmoid(gate_pre)
    hidden = (gate_pre * squash * up_pre).astype(jnp.bfloat16)
    grad_hidden = lax.dot_general(rows_cot, down_rows, contract, preferred_element_type=jnp.float32)
    grad_gate = (grad_hidden * up_pre * squash * (1.0 + gate_pre * (1.0 - squash))).astype(
        jnp.bfloat16
    )
    grad_up = (grad_hidden * gate_pre * squash).astype(jnp.bfloat16)
    part_out = jnp.dot(hidden, down_rows, preferred_element_type=jnp.float32)
    partial_gradient = lax.dot_general(
        grad_gate, gate_cols, contract, preferred_element_type=jnp.float32
    )
    partial_gradient = partial_gradient + lax.dot_general(
        grad_up, up_cols, contract, preferred_element_type=jnp.float32
    )
    return (part_out, partial_gradient)


def shared_rows(input_rows, rows_cot, gate_cols, up_cols, down_rows):
    every_in, every_cot = (
        lax.all_gather(input_rows, "dp", axis=0, tiled=True),
        lax.all_gather(rows_cot, "dp", axis=0, tiled=True),
    )
    part_out, partial_gradient = expert_pass(every_in, every_cot, gate_cols, up_cols, down_rows)
    summed_out, summed_grad = (
        lax.psum_scatter(
            part_out.astype(jnp.bfloat16), "dp", scatter_dimension=0, tiled=True
        ).astype(jnp.float32),
        lax.psum_scatter(
            partial_gradient.astype(jnp.bfloat16), "dp", scatter_dimension=0, tiled=True
        ).astype(jnp.float32),
    )
    return (summed_out.astype(jnp.bfloat16), summed_grad.astype(jnp.bfloat16))


def shards(acts, cotangent, routes, probs, keep, w_gate, w_up, w_down):
    n_expert = lax.axis_size("expert")
    experts = n_expert // 2
    token_count = acts.shape[0]
    width = acts.shape[1]
    top_count = routes.shape[1]
    capacity = 2 * ((token_count * top_count * 5 + 8 * experts - 1) // (8 * experts))
    slot_count = experts * capacity
    pair_count = token_count * top_count
    chosen = routes.reshape(pair_count)
    weights = probs.reshape(pair_count)
    expert_hot = (chosen[:, None] == jnp.arange(experts, dtype=jnp.int32)[None, :]).astype(
        jnp.int32
    )
    ranks = jnp.cumsum(expert_hot, axis=0) - 1
    placed = jnp.sum(expert_hot * ranks, axis=1)
    target = chosen * capacity + placed
    slot_hot = target[:, None] == jnp.arange(slot_count, dtype=jnp.int32)[None, :]
    owner = jnp.arange(pair_count, dtype=jnp.int32) // top_count
    token_hot = (owner[:, None] == jnp.arange(token_count, dtype=jnp.int32)[None, :]).astype(
        jnp.bfloat16
    )
    scatter_mat = jnp.dot(
        slot_hot.astype(jnp.bfloat16).T, token_hot, preferred_element_type=jnp.float32
    ).astype(jnp.bfloat16)
    weighted_hot = jnp.where(slot_hot, weights[:, None], jnp.zeros((), jnp.bfloat16))
    gather_matrix = jnp.dot(token_hot.T, weighted_hot, preferred_element_type=jnp.float32).astype(
        jnp.bfloat16
    )
    packed_in = jnp.dot(scatter_mat, acts, preferred_element_type=jnp.float32).astype(jnp.bfloat16)
    packed_cot = jnp.dot(scatter_mat, cotangent, preferred_element_type=jnp.float32).astype(
        jnp.bfloat16
    )
    gate_cols = w_gate[0, 0]
    up_cols = w_up[0, 0]
    down_rows = w_down[0, 0]
    send_in = jnp.repeat(packed_in.reshape(experts, capacity, width), 2, axis=0).reshape(
        n_expert * capacity, width
    )
    send_cot = jnp.repeat(packed_cot.reshape(experts, capacity, width), 2, axis=0).reshape(
        n_expert * capacity, width
    )
    got_in, got_cot = (
        lax.all_to_all(send_in, "expert", split_axis=0, concat_axis=0, tiled=True),
        lax.all_to_all(send_cot, "expert", split_axis=0, concat_axis=0, tiled=True),
    )
    half_out, half_grad = shared_rows(got_in, got_cot, gate_cols, up_cols, down_rows)
    back_out, back_grad = (
        lax.all_to_all(half_out, "expert", split_axis=0, concat_axis=0, tiled=True),
        lax.all_to_all(half_grad, "expert", split_axis=0, concat_axis=0, tiled=True),
    )
    expert_out = jnp.sum(back_out.reshape(experts, 2, capacity, width).astype(jnp.float32), axis=1)
    expert_out = expert_out.astype(jnp.bfloat16).reshape(slot_count, width)
    expert_grad = jnp.sum(
        back_grad.reshape(experts, 2, capacity, width).astype(jnp.float32), axis=1
    )
    expert_grad = expert_grad.astype(jnp.bfloat16).reshape(slot_count, width)
    mixed_out = jnp.dot(gather_matrix, expert_out, preferred_element_type=jnp.float32)
    mixed_grad = jnp.dot(gather_matrix, expert_grad, preferred_element_type=jnp.float32)
    keep_scale = keep[0, 0].astype(jnp.float32)
    layer_out = (acts.astype(jnp.float32) + keep_scale * mixed_out).astype(jnp.bfloat16)
    section_grad = (cotangent.astype(jnp.float32) + keep_scale * mixed_grad).astype(jnp.bfloat16)
    grad_below = from_behind(section_grad, "pipe", -1)
    return (layer_out, grad_below)


def solution(mesh):
    return jax.shard_map(
        shards,
        mesh=mesh,
        in_specs=(
            P(("pipe", "expert", "dp"), None),
            P(("pipe", "expert", "dp"), None),
            P(("pipe", "expert", "dp"), None),
            P(("pipe", "expert", "dp"), None),
            P("pipe", ("expert", "dp")),
            P("pipe", "expert", None, "dp"),
            P("pipe", "expert", None, "dp"),
            P("pipe", "expert", "dp", None),
        ),
        out_specs=(P(("pipe", "expert", "dp"), None), P(("pipe", "expert", "dp"), None)),
        check_vma=False,
    )
```

profile of v0, /device:TPU:0, one launch (start us, length us, event | category | flops | bytes accessed | tf_op | source)
XLA Modules:
  0.0 100.5 jit_solution(3909824233218656353)
XLA Ops:
  7.2 0.0 copy-start
  7.2 0.8 fusion.24
  8.0 0.2 reduce_window_sum.11
  8.2 0.7 select_reduce_fusion
  8.8 0.7 fusion.25
  9.5 0.2 convolution_convert_fusion.4
  9.7 1.0 %convolution_convert_fusion.2 = bf16[12,3584]{1,0:T(8,128)(2,1)S(1)} fusion(bf16[12,8]{0,1:T(8,128)(2,1)S(1)} %convolution_convert_fusion.4, bf16[8,3584]{1,0:T(8,128)(2,1)} %param.8), kind=kOutput, calls=%fused_computation.4 | convolution fusion | flops 731136 | bytes 143552 | tf_op jit(solution)/shard_map/dot_general | solution.py:80
  10.8 0.7 broadcast_in_dim.28
  11.5 6.3 %all-to-all-start = ((bf16[4,6,3584]{2,1,0:T(8,128)(2,1)}), bf16[4,6,3584]{2,1,0:T(8,128)(2,1)S(1)}, u32[]{:S(2)}, u32[]{:S(2)}) async-start(bf16[4,6,3584]{2,1,0:T(8,128)(2,1)} %bitcast.5), calls=%async_computation | async-start | bytes 458752 | tf_op jit(solution)/shard_map/all_to_all | solution.py:94
  17.8 1.0 %convolution_convert_fusion.1 = bf16[12,3584]{1,0:T(8,128)(2,1)S(1)} fusion(bf16[12,8]{0,1:T(8,128)(2,1)S(1)} %convolution_convert_fusion.4, bf16[8,3584]{1,0:T(8,128)(2,1)} %param.9), kind=kOutput, calls=%fused_computation.3 | convolution fusion | flops 731136 | bytes 143552 | tf_op jit(solution)/shard_map/dot_general | solution.py:81
  18.9 7.1 %all-to-all-done = bf16[4,6,3584]{2,1,0:T(8,128)(2,1)S(1)} async-done(((bf16[4,6,3584]{2,1,0:T(8,128)(2,1)}), bf16[4,6,3584]{2,1,0:T(8,128)(2,1)S(1)}, u32[]{:S(2)}, u32[]{:S(2)}) %all-to-all-start) | async-done | bytes 172064 | tf_op jit(solution)/shard_map/all_to_all | solution.py:94
  26.0 0.7 broadcast_in_dim.29
  26.7 3.4 %all-to-all-start.2 = ((bf16[4,6,3584]{2,1,0:T(8,128)(2,1)}), bf16[4,6,3584]{2,1,0:T(8,128)(2,1)S(1)}, u32[]{:S(2)}, u32[]{:S(2)}) async-start(bf16[4,6,3584]{2,1,0:T(8,128)(2,1)} %bitcast.10), calls=%async_computation.3 | async-start | bytes 458752 | tf_op jit(solution)/shard_map/all_to_all | solution.py:95
  30.1 0.0 reduce-scatter.5.cloned.1.call-start
  30.1 0.1 all_to_all.30
  30.2 0.0 copy-start.1
  30.2 6.2 %all_gather.6 = bf16[48,3584]{1,0:T(8,128)(2,1)S(1)} all-gather(bf16[24,3584]{1,0:T(8,128)(2,1)S(1)} %all_to_all.30), channel_id=1, replica_groups=mesh['pipe'=4,'expert'=4,'dp'=2] {'dp'}, dimensions={0}, use_global_device_ids=true | all-gather | bytes 516096 | tf_op jit(solution)/shard_map/all_gather | solution.py:36
  36.4 0.0 copy-done
  36.4 0.4 fusion.13
  36.9 0.0 copy-done.1
  36.9 0.4 fusion.9
  37.3 0.0 all-to-all-done.2
  37.3 0.1 all_to_all.35
  37.4 6.1 %all_gather.7 = bf16[48,3584]{1,0:T(8,128)(2,1)S(1)} all-gather(bf16[24,3584]{1,0:T(8,128)(2,1)S(1)} %all_to_all.35), channel_id=1, replica_groups=mesh['pipe'=4,'expert'=4,'dp'=2] {'dp'}, dimensions={0}, use_global_device_ids=true | all-gather | bytes 516096 | tf_op jit(solution)/shard_map/all_gather | solution.py:37
  43.5 2.1 %fusion.5 = f32[48,256]{1,0:T(8,128)S(1)} fusion(bf16[48,3584]{1,0:T(8,128)(2,1)S(1)} %all_gather.7, bf16[1,1,256,3584]{3,2,1,0:T(8,128)(2,1)} %param.15), kind=kOutput, calls=%fused_computation.11 | convolution fusion | flops 88080384 | bytes 2228224 | tf_op jit(solution)/shard_map/dot_general | solution.py:19
  45.6 0.0 copy-start.2
  45.6 0.6 fusion.11
  46.3 0.9 copy-done.2
  47.1 1.4 %fusion = bf16[48,3584]{1,0:T(8,128)(2,1)} fusion(f32[48,3584]{1,0:T(8,128)S(1)} %fusion.11, bf16[1,1,3584,256]{3,2,1,0:T(8,128)(2,1)S(1)} %copy-done.2, f32[48,256]{1,0:T(8,128)S(1)} %fusion.5, f32[48,256]{1,0:T(8,128)S(1)} %fusion.13), kind=kOutput, calls=%fused_computation.1 | convolution fusion | flops 88498176 | bytes 2965504 | tf_op jit(solution)/shard_map/dot_general | solution.py:28
  48.5 0.0 copy-start.5
  48.5 0.0 reduce-scatter.5.cloned.1.call-update
  48.6 0.0 reduce-scatter.3.cloned.1.call-start
  48.6 2.6 %convolution_convert_fusion = bf16[48,3584]{1,0:T(8,128)(2,1)} fusion(bf16[1,1,256,3584]{3,2,1,0:T(8,128)(2,1)} %param.15, f32[48,256]{1,0:T(8,128)S(1)} %fusion.9, f32[48,256]{1,0:T(8,128)S(1)} %fusion.13), kind=kOutput, calls=%fused_computation.2 | convolution fusion | flops 88326144 | bytes 2277376 | tf_op jit(solution)/shard_map/dot_general | solution.py:24
  51.2 0.0 copy-start.3
  51.2 0.0 copy-start.4
  51.2 0.0 reduce-scatter.3.cloned.1.call-update
  51.3 11.4 %reduce-scatter.5.cloned.1.call-done = bf16[24,3584]{1,0:T(8,128)(2,1)} async-done(((bf16[48,3584]{1,0:T(8,128)(2,1)}), bf16[24,3584]{1,0:T(8,128)(2,1)}) %reduce-scatter.5.cloned.1.call-update) | async-done | bytes 172048 | tf_op jit(solution)/shard_map/reduce_scatter | solution.py:44
  62.7 1.7 %all_to_all.36 = bf16[4,6,3584]{2,1,0:T(8,128)(2,1)} reshape(bf16[24,3584]{1,0:T(8,128)(2,1)} %reduce-scatter.5.cloned.1.call-done) | data formatting | bytes 344064 | tf_op jit(solution)/shard_map/all_to_all | solution.py:100
  64.3 4.6 %all-to-all-start.3 = ((bf16[4,6,3584]{2,1,0:T(8,128)(2,1)}), bf16[4,6,3584]{2,1,0:T(8,128)(2,1)S(1)}, u32[]{:S(2)}, u32[]{:S(2)}) async-start(bf16[4,6,3584]{2,1,0:T(8,128)(2,1)} %all_to_all.36), calls=%async_computation.5 | async-start | bytes 458752 | tf_op jit(solution)/shard_map/all_to_all | solution.py:100
  69.6 0.0 copy-done.5
  69.6 0.2 convolution_convert_fusion.3
  69.8 7.9 %reduce-scatter.3.cloned.1.call-done = bf16[24,3584]{1,0:T(8,128)(2,1)} async-done(((bf16[48,3584]{1,0:T(8,128)(2,1)}), bf16[24,3584]{1,0:T(8,128)(2,1)}) %reduce-scatter.3.cloned.1.call-update) | async-done | bytes 172048 | tf_op jit(solution)/shard_map/reduce_scatter | solution.py:41
  77.6 1.7 %all_to_all.31 = bf16[4,6,3584]{2,1,0:T(8,128)(2,1)} reshape(bf16[24,3584]{1,0:T(8,128)(2,1)} %reduce-scatter.3.cloned.1.call-done) | data formatting | bytes 344064 | tf_op jit(solution)/shard_map/all_to_all | solution.py:99
  79.3 0.0 all-to-all-done.3
  79.3 4.6 %all-to-all-start.1 = ((bf16[4,6,3584]{2,1,0:T(8,128)(2,1)}), bf16[4,6,3584]{2,1,0:T(8,128)(2,1)S(1)}, u32[]{:S(2)}, u32[]{:S(2)}) async-start(bf16[4,6,3584]{2,1,0:T(8,128)(2,1)} %all_to_all.31), calls=%async_computation.2 | async-start | bytes 458752 | tf_op jit(solution)/shard_map/all_to_all | solution.py:99
  84.0 0.0 copy-done.3
  84.0 0.1 fusion.4
  84.1 1.3 %collective-permute-start = (bf16[8,3584]{1,0:T(8,128)(2,1)S(1)}, bf16[8,3584]{1,0:T(8,128)(2,1)S(1)}, u32[]{:S(2)}, u32[]{:S(2)}) collective-permute-start(bf16[8,3584]{1,0:T(8,128)(2,1)S(1)} %fusion.4), channel_id=1, source_target_pairs={{8,0},{16,8},{24,16},{9,1},{17,9},{25,17},{10,2},{18,10},{26,18},{... | collective-permute-start | bytes 172040 | tf_op jit(solution)/shard_map/ppermute | solution.py:10
  85.4 6.7 %all-to-all-done.1 = bf16[4,6,3584]{2,1,0:T(8,128)(2,1)S(1)} async-done(((bf16[4,6,3584]{2,1,0:T(8,128)(2,1)}), bf16[4,6,3584]{2,1,0:T(8,128)(2,1)S(1)}, u32[]{:S(2)}, u32[]{:S(2)}) %all-to-all-start.1) | async-done | bytes 172064 | tf_op jit(solution)/shard_map/all_to_all | solution.py:99
  92.2 0.0 copy-done.4
  92.2 0.8 fusion.3
  93.0 0.0 collective-permute-done
  93.0 0.6 copy.12
  (6 shorter events, 0.2 us)
Async XLA Ops:
  7.2 29.3 %copy-start = (bf16[1,1,3584,256]{3,2,1,0:T(8,128)(2,1)S(1)}, bf16[1,1,3584,256]{3,2,1,0:T(8,128)(2,1)}, u32[]{:S(2)}) copy-start(bf16[1,1,3584,256]{3,2,1,0:T(8,128)(2,1)} %param.13) | copy-start | bytes 5505028
  11.5 14.5 %all-to-all-start = ((bf16[4,6,3584]{2,1,0:T(8,128)(2,1)}), bf16[4,6,3584]{2,1,0:T(8,128)(2,1)S(1)}, u32[]{:S(2)}, u32[]{:S(2)}) async-start(bf16[4,6,3584]{2,1,0:T(8,128)(2,1)} %bitcast.5), calls=%async_computation | async-start | bytes 458752 | tf_op jit(solution)/shard_map/all_to_all | solution.py:94
  26.7 10.6 %all-to-all-start.2 = ((bf16[4,6,3584]{2,1,0:T(8,128)(2,1)}), bf16[4,6,3584]{2,1,0:T(8,128)(2,1)S(1)}, u32[]{:S(2)}, u32[]{:S(2)}) async-start(bf16[4,6,3584]{2,1,0:T(8,128)(2,1)} %bitcast.10), calls=%async_computation.3 | async-start | bytes 458752 | tf_op jit(solution)/shard_map/all_to_all | solution.py:95
  30.1 32.6 %reduce-scatter.5.cloned.1.call-start = ((), (), s32[]{:S(2)}) async-start(), calls=%async_computation.7 | async-start | bytes 516096 | tf_op jit(solution)/shard_map/reduce_scatter | solution.py:44
  30.2 6.7 %copy-start.1 = (bf16[1,1,3584,256]{3,2,1,0:T(8,128)(2,1)S(1)}, bf16[1,1,3584,256]{3,2,1,0:T(8,128)(2,1)}, u32[]{:S(2)}) copy-start(bf16[1,1,3584,256]{3,2,1,0:T(8,128)(2,1)} %param.14) | copy-start | bytes 5505028
  45.6 1.5 %copy-start.2 = (bf16[1,1,3584,256]{3,2,1,0:T(8,128)(2,1)S(1)}, bf16[1,1,3584,256]{3,2,1,0:T(8,128)(2,1)}, u32[]{:S(2)}) copy-start(bf16[1,1,3584,256]{3,2,1,0:T(8,128)(2,1)} %param.14) | copy-start | bytes 5505028
  48.5 21.1 %copy-start.5 = (bf16[8,1]{0,1:T(2,128)(2,1)S(1)}, bf16[8,1]{0,1:T(2,128)(2,1)}, u32[]{:S(2)}) copy-start(bf16[8,1]{0,1:T(2,128)(2,1)} %param.11) | copy-start | bytes 52
  48.6 29.1 %reduce-scatter.3.cloned.1.call-start = ((), (), s32[]{:S(2)}) async-start(), calls=%async_computation.6 | async-start | bytes 516096 | tf_op jit(solution)/shard_map/reduce_scatter | solution.py:41
  51.2 32.8 %copy-start.3 = (bf16[8,3584]{1,0:T(8,128)(2,1)S(1)}, bf16[8,3584]{1,0:T(8,128)(2,1)}, u32[]{:S(2)}) copy-start(bf16[8,3584]{1,0:T(8,128)(2,1)} %param.9) | copy-start | bytes 172036
  51.2 41.0 %copy-start.4 = (bf16[8,3584]{1,0:T(8,128)(2,1)S(1)}, bf16[8,3584]{1,0:T(8,128)(2,1)}, u32[]{:S(2)}) copy-start(bf16[8,3584]{1,0:T(8,128)(2,1)} %param.8) | copy-start | bytes 172036
  64.3 14.9 %all-to-all-start.3 = ((bf16[4,6,3584]{2,1,0:T(8,128)(2,1)}), bf16[4,6,3584]{2,1,0:T(8,128)(2,1)S(1)}, u32[]{:S(2)}, u32[]{:S(2)}) async-start(bf16[4,6,3584]{2,1,0:T(8,128)(2,1)} %all_to_all.36), calls=%async_computation.5 | async-start | bytes 458752 | tf_op jit(solution)/shard_map/all_to_all | solution.py:100
  79.3 12.8 %all-to-all-start.1 = ((bf16[4,6,3584]{2,1,0:T(8,128)(2,1)}), bf16[4,6,3584]{2,1,0:T(8,128)(2,1)S(1)}, u32[]{:S(2)}, u32[]{:S(2)}) async-start(bf16[4,6,3584]{2,1,0:T(8,128)(2,1)} %all_to_all.31), calls=%async_computation.2 | async-start | bytes 458752 | tf_op jit(solution)/shard_map/all_to_all | solution.py:99
  84.1 8.8 %collective-permute-start = (bf16[8,3584]{1,0:T(8,128)(2,1)S(1)}, bf16[8,3584]{1,0:T(8,128)(2,1)S(1)}, u32[]{:S(2)}, u32[]{:S(2)}) collective-permute-start(bf16[8,3584]{1,0:T(8,128)(2,1)S(1)} %fusion.4), channel_id=1, source_target_pairs={{8,0},{16,8},{24,16},{9,1},{17,9},{25,17},{10,2},{18,10},{26,18},{... | collective-permute-start | bytes 172040 | tf_op jit(solution)/shard_map/ppermute | solution.py:10
Sparse Core Ops, SparseCore 0:
  48.7 13.9 reduce-scatter.4
  64.9 12.6 reduce-scatter.2
where the time goes:
time: 101 us; the launch traced here: 100 us
  waiting for transfers between devices  33.1 us (33%)
  starting transfers between devices  20.3 us (20%)
  between operations  14.9 us (15%)
  blocking collectives  12.3 us (12%)
  matrix products  11 us (11%)
  local copies, waits for them, and re-layouts  6.49 us (6%)
  other arithmetic  2.4 us (2%)
    reduce_scatter x1, waiting for transfers between devices, shared_rows(): lax.psum_scatter(partial_gradient.astype(jnp.bfloat16), 'dp', scatter_dim...  11.4 us
    reduce_scatter x1, waiting for transfers between devices, shared_rows(): lax.psum_scatter(part_out.astype(jnp.bfloat16), 'dp', scatter_dimension=0...  7.88 us
    all_to_all x1, waiting for transfers between devices, shards(): lax.all_to_all(send_in, 'expert', split_axis=0, concat_axis=0, tiled=True)  7.13 us
    all_to_all x1, waiting for transfers between devices, shards(): lax.all_to_all(half_out, 'expert', split_axis=0, concat_axis=0, tiled=True)  6.68 us
    all_to_all x1, starting transfers between devices, shards(): lax.all_to_all(send_in, 'expert', split_axis=0, concat_axis=0, tiled=True)  6.32 us
    all_gather x1, blocking collectives, shared_rows(): lax.all_gather(input_rows, 'dp', axis=0, tiled=True)  6.22 us
    all_gather x1, blocking collectives, shared_rows(): lax.all_gather(rows_cot, 'dp', axis=0, tiled=True)  6.08 us
    all_to_all x1, starting transfers between devices, shards(): lax.all_to_all(half_out, 'expert', split_axis=0, concat_axis=0, tiled=True)  4.61 us
  transfers between devices with their start and end apart: 7, of which 4 were waited for; matrix products, arithmetic and copies ran while one was open for 6% of the time, Pallas kernels for 0%

commit v1 on v0

--- a/solution.py
+++ b/solution.py
@@ -2,6 +2,18 @@
 import jax.numpy as jnp
 from jax import lax
 from jax.sharding import PartitionSpec as P
+
+
+def exchange_directly(shard, axis, split, join):
+    ways, here = (lax.axis_size(axis), lax.axis_index(axis))
+    width = shard.shape[split] // ways
+    turned = jnp.roll(shard, -here * width, axis=split)
+    got = [lax.slice_in_dim(turned, 0, width, axis=split)]
+    for far in range(1, ways):
+        sent = lax.slice_in_dim(turned, far * width, (far + 1) * width, axis=split)
+        got.append(lax.ppermute(sent, axis, [(d, (d + far) % ways) for d in range(ways)]))
+    line = jnp.concatenate(got[::-1], axis=join)
+    return jnp.roll(line, (here + 1) * got[0].shape[join], axis=join)
 
 
 def from_behind(shard, axis, by):
@@ -92,7 +104,7 @@
     )
     got_in, got_cot = (
         lax.all_to_all(send_in, "expert", split_axis=0, concat_axis=0, tiled=True),
-        lax.all_to_all(send_cot, "expert", split_axis=0, concat_axis=0, tiled=True),
+        exchange_directly(send_cot, "expert", 0, 0),
     )
     half_out, half_grad = shared_rows(got_in, got_cot, gate_cols, up_cols, down_rows)
     back_out, back_grad = (

time: 101 us -> 93 us (0.921)
  waiting for transfers between devices: 33.1 us -> 25.9 us
  local copies, waits for them, and re-layouts: 6.49 us -> 4.99 us
    all_to_all x1, waiting for transfers between devices: 7.13 us -> 0.01 us  [shards(): lax.all_to_all(send_in, 'expert', split_axis=0, concat_axis=0, tiled=True)]
    ppermute x0 -> x3, starting transfers between devices: none -> 6.11 us  [exchange_directly(): lax.ppermute(sent, axis, [(d, (d + far) % ways) for d in range(ways)])]
    all_to_all x1 -> x0, starting transfers between devices: 3.38 us -> none  [shards(): lax.all_to_all(send_cot, 'expert', split_axis=0, concat_axis=0, tiled=True)]
    all_to_all x1, starting transfers between devices: 6.32 us -> 4.08 us  [shards(): lax.all_to_all(send_in, 'expert', split_axis=0, concat_axis=0, tiled=True)]
  transfers between devices with their start and end apart: 7 -> 9, of which waited for: 4 -> 3; matrix products, arithmetic and copies ran while one was open for 6% -> 8% of each run, Pallas kernels for 0% -> 0%
where the time goes in v1:
time: 93 us; the launch traced here: 92.4 us
  waiting for transfers between devices  25.9 us (28%)
  starting transfers between devices  20.7 us (22%)
  between operations  14.9 us (16%)
  blocking collectives  12.3 us (13%)
  matrix products  10.2 us (11%)
  local copies, waits for them, and re-layouts  4.99 us (5%)
  other arithmetic  3.31 us (4%)
    reduce_scatter x1, waiting for transfers between devices, shared_rows(): lax.psum_scatter(partial_gradient.astype(jnp.bfloat16), 'dp', scatter_dim...  11.5 us
    reduce_scatter x1, waiting for transfers between devices, shared_rows(): lax.psum_scatter(part_out.astype(jnp.bfloat16), 'dp', scatter_dimension=0...  7.77 us
    all_to_all x1, waiting for transfers between devices, shards(): lax.all_to_all(half_out, 'expert', split_axis=0, concat_axis=0, tiled=True)  6.67 us
    all_gather x1, blocking collectives, shared_rows(): lax.all_gather(input_rows, 'dp', axis=0, tiled=True)  6.22 us
    ppermute x3, starting transfers between devices, exchange_directly(): lax.ppermute(sent, axis, [(d, (d + far) % ways) for d in range(ways)])  6.11 us
    all_gather x1, blocking collectives, shared_rows(): lax.all_gather(rows_cot, 'dp', axis=0, tiled=True)  6.08 us
    all_to_all x1, starting transfers between devices, shards(): lax.all_to_all(half_grad, 'expert', split_axis=0, concat_axis=0, tiled=True)  4.61 us
    all_to_all x1, starting transfers between devices, shards(): lax.all_to_all(half_out, 'expert', split_axis=0, concat_axis=0, tiled=True)  4.61 us
  transfers between devices with their start and end apart: 9, of which 3 were waited for; matrix products, arithmetic and copies ran while one was open for 8% of the time, Pallas kernels for 0%

profile of v1, /device:TPU:0, one launch (start us, length us, event | category | flops | bytes accessed | tf_op | source)
XLA Modules:
  0.0 92.4 jit_solution(9195618538789516800)
XLA Ops:
  7.2 0.0 copy-start
  7.2 0.0 copy-start.3
  7.2 0.8 fusion.32
  8.0 0.2 reduce_window_sum.11
  8.2 0.7 select_reduce_fusion
  8.9 0.7 fusion.33
  9.5 0.2 convolution_convert_fusion.4
  9.7 1.0 %convolution_convert_fusion.1 = bf16[12,3584]{1,0:T(8,128)(2,1)S(1)} fusion(bf16[12,8]{0,1:T(8,128)(2,1)S(1)} %convolution_convert_fusion.4, bf16[8,3584]{1,0:T(8,128)(2,1)} %param.11), kind=kOutput, calls=%fused_computation.3 | convolution fusion | flops 731136 | bytes 143552 | tf_op jit(solution)/shard_map/dot_general | solution.py:93
  10.8 0.1 reshape_reshape.4
  10.9 0.1 fusion.22
  11.1 5.1 %collective-permute-start = (bf16[6,3584]{1,0:T(8,128)(2,1)S(1)}, bf16[6,3584]{1,0:T(8,128)(2,1)S(1)}, u32[]{:S(2)}, u32[]{:S(2)}) collective-permute-start(bf16[6,3584]{1,0:T(8,128)(2,1)S(1)} %get-tuple-element.6), channel_id=1, source_target_pairs={{0,6},{2,0},{4,2},{6,4},{1,7},{3,1},{5,3},{7,5},{8,14},{10,8},{12,... | collective-permute-start | bytes 129032 | tf_op jit(solution)/shard_map/ppermute | solution.py:14
  16.2 0.0 collective-permute-start.1
  16.2 1.0 %collective-permute-start.2 = (bf16[6,3584]{1,0:T(8,128)(2,1)S(1)}, bf16[6,3584]{1,0:T(8,128)(2,1)S(1)}, u32[]{:S(2)}, u32[]{:S(2)}) collective-permute-start(bf16[6,3584]{1,0:T(8,128)(2,1)S(1)} %get-tuple-element.4), channel_id=1, source_target_pairs={{0,2},{2,4},{4,6},{6,0},{1,3},{3,5},{5,7},{7,1},{8,10},{10,12},{12... | collective-permute-start | bytes 129032 | tf_op jit(solution)/shard_map/ppermute | solution.py:14
  17.2 0.0 copy-done.3
  17.2 0.2 convolution_convert_fusion.2
  17.5 0.7 broadcast_in_dim.28
  18.2 4.1 %all-to-all-start = ((bf16[4,6,3584]{2,1,0:T(8,128)(2,1)}), bf16[4,6,3584]{2,1,0:T(8,128)(2,1)S(1)}, u32[]{:S(2)}, u32[]{:S(2)}) async-start(bf16[4,6,3584]{2,1,0:T(8,128)(2,1)} %bitcast.5), calls=%async_computation | async-start | bytes 458752 | tf_op jit(solution)/shard_map/all_to_all | solution.py:106
  22.3 0.0 reduce-scatter.5.cloned.1.call-start
  22.3 0.0 collective-permute-done
  22.3 0.0 collective-permute-done.1
  22.3 0.0 collective-permute-done.2
  22.3 0.8 fusion.18
  23.1 6.1 %all_gather.7 = bf16[48,3584]{1,0:T(8,128)(2,1)S(1)} all-gather(bf16[24,3584]{1,0:T(8,128)(2,1)S(1)} %fusion.18), channel_id=1, replica_groups=mesh['pipe'=4,'expert'=4,'dp'=2] {'dp'}, dimensions={0}, use_global_device_ids=true | all-gather | bytes 516096 | tf_op jit(solution)/shard_map/all_gather | solution.py:49
  29.2 2.1 %fusion.5 = f32[48,256]{1,0:T(8,128)S(1)} fusion(bf16[48,3584]{1,0:T(8,128)(2,1)S(1)} %all_gather.7, bf16[1,1,256,3584]{3,2,1,0:T(8,128)(2,1)} %param.17), kind=kOutput, calls=%fused_computation.11 | convolution fusion | flops 88080384 | bytes 2228224 | tf_op jit(solution)/shard_map/dot_general | solution.py:31
  31.3 0.0 all-to-all-done
  31.3 0.1 all_to_all.22
  31.4 0.0 copy-start.1
  31.4 6.2 %all_gather.6 = bf16[48,3584]{1,0:T(8,128)(2,1)S(1)} all-gather(bf16[24,3584]{1,0:T(8,128)(2,1)S(1)} %all_to_all.22), channel_id=1, replica_groups=mesh['pipe'=4,'expert'=4,'dp'=2] {'dp'}, dimensions={0}, use_global_device_ids=true | all-gather | bytes 516096 | tf_op jit(solution)/shard_map/all_gather | solution.py:48
  37.6 0.0 copy-done
  37.6 0.4 fusion.13
  38.0 0.0 copy-done.1
  38.1 0.4 fusion.9
  38.5 0.6 fusion.11
  39.1 1.4 %fusion = bf16[48,3584]{1,0:T(8,128)(2,1)} fusion(f32[48,3584]{1,0:T(8,128)S(1)} %fusion.11, bf16[1,1,3584,256]{3,2,1,0:T(8,128)(2,1)S(1)} %copy-done.1, f32[48,256]{1,0:T(8,128)S(1)} %fusion.5, f32[48,256]{1,0:T(8,128)S(1)} %fusion.13), kind=kOutput, calls=%fused_computation.1 | convolution fusion | flops 88498176 | bytes 2965504 | tf_op jit(solution)/shard_map/dot_general | solution.py:40
  40.5 0.0 copy-start.4
  40.5 0.0 reduce-scatter.5.cloned.1.call-update
  40.6 0.0 reduce-scatter.3.cloned.1.call-start
  40.6 2.6 %convolution_convert_fusion = bf16[48,3584]{1,0:T(8,128)(2,1)} fusion(bf16[1,1,256,3584]{3,2,1,0:T(8,128)(2,1)} %param.17, f32[48,256]{1,0:T(8,128)S(1)} %fusion.9, f32[48,256]{1,0:T(8,128)S(1)} %fusion.13), kind=kOutput, calls=%fused_computation.2 | convolution fusion | flops 88326144 | bytes 2277376 | tf_op jit(solution)/shard_map/dot_general | solution.py:36
  43.3 0.0 copy-start.2
  43.3 0.0 reduce-scatter.3.cloned.1.call-update
  43.3 11.5 %reduce-scatter.5.cloned.1.call-done = bf16[24,3584]{1,0:T(8,128)(2,1)} async-done(((bf16[48,3584]{1,0:T(8,128)(2,1)}), bf16[24,3584]{1,0:T(8,128)(2,1)}) %reduce-scatter.5.cloned.1.call-update) | async-done | bytes 172048 | tf_op jit(solution)/shard_map/reduce_scatter | solution.py:56
  54.7 1.7 %all_to_all.25 = bf16[4,6,3584]{2,1,0:T(8,128)(2,1)} reshape(bf16[24,3584]{1,0:T(8,128)(2,1)} %reduce-scatter.5.cloned.1.call-done) | data formatting | bytes 344064 | tf_op jit(solution)/shard_map/all_to_all | solution.py:112
  56.4 4.6 %all-to-all-start.2 = ((bf16[4,6,3584]{2,1,0:T(8,128)(2,1)}), bf16[4,6,3584]{2,1,0:T(8,128)(2,1)S(1)}, u32[]{:S(2)}, u32[]{:S(2)}) async-start(bf16[4,6,3584]{2,1,0:T(8,128)(2,1)} %all_to_all.25), calls=%async_computation.4 | async-start | bytes 458752 | tf_op jit(solution)/shard_map/all_to_all | solution.py:112
  61.7 0.0 copy-done.4
  61.7 0.2 convolution_convert_fusion.3
  61.8 7.8 %reduce-scatter.3.cloned.1.call-done = bf16[24,3584]{1,0:T(8,128)(2,1)} async-done(((bf16[48,3584]{1,0:T(8,128)(2,1)}), bf16[24,3584]{1,0:T(8,128)(2,1)}) %reduce-scatter.3.cloned.1.call-update) | async-done | bytes 172048 | tf_op jit(solution)/shard_map/reduce_scatter | solution.py:53
  69.6 1.7 %all_to_all.23 = bf16[4,6,3584]{2,1,0:T(8,128)(2,1)} reshape(bf16[24,3584]{1,0:T(8,128)(2,1)} %reduce-scatter.3.cloned.1.call-done) | data formatting | bytes 344064 | tf_op jit(solution)/shard_map/all_to_all | solution.py:111
  71.3 0.0 all-to-all-done.2
  71.3 4.6 %all-to-all-start.1 = ((bf16[4,6,3584]{2,1,0:T(8,128)(2,1)}), bf16[4,6,3584]{2,1,0:T(8,128)(2,1)S(1)}, u32[]{:S(2)}, u32[]{:S(2)}) async-start(bf16[4,6,3584]{2,1,0:T(8,128)(2,1)} %all_to_all.23), calls=%async_computation.2 | async-start | bytes 458752 | tf_op jit(solution)/shard_map/all_to_all | solution.py:111
  76.0 0.0 copy-done.2
  76.0 0.1 fusion.4
  76.1 1.3 %collective-permute-start.3 = (bf16[8,3584]{1,0:T(8,128)(2,1)S(1)}, bf16[8,3584]{1,0:T(8,128)(2,1)S(1)}, u32[]{:S(2)}, u32[]{:S(2)}) collective-permute-start(bf16[8,3584]{1,0:T(8,128)(2,1)S(1)} %fusion.4), channel_id=1, source_target_pairs={{8,0},{16,8},{24,16},{9,1},{17,9},{25,17},{10,2},{18,10},{26,18},{... | collective-permute-start | bytes 172040 | tf_op jit(solution)/shard_map/ppermute | solution.py:22
  77.4 6.7 %all-to-all-done.1 = bf16[4,6,3584]{2,1,0:T(8,128)(2,1)S(1)} async-done(((bf16[4,6,3584]{2,1,0:T(8,128)(2,1)}), bf16[4,6,3584]{2,1,0:T(8,128)(2,1)S(1)}, u32[]{:S(2)}, u32[]{:S(2)}) %all-to-all-start.1) | async-done | bytes 172064 | tf_op jit(solution)/shard_map/all_to_all | solution.py:111
  84.2 0.8 fusion.3
  85.0 0.0 collective-permute-done.3
  85.0 0.6 copy.12
  (8 shorter events, 0.3 us)
Async XLA Ops:
  7.2 30.4 %copy-start = (bf16[1,1,3584,256]{3,2,1,0:T(8,128)(2,1)S(1)}, bf16[1,1,3584,256]{3,2,1,0:T(8,128)(2,1)}, u32[]{:S(2)}) copy-start(bf16[1,1,3584,256]{3,2,1,0:T(8,128)(2,1)} %param.15) | copy-start | bytes 5505028
  7.2 10.0 %copy-start.3 = (bf16[8,3584]{1,0:T(8,128)(2,1)S(1)}, bf16[8,3584]{1,0:T(8,128)(2,1)}, u32[]{:S(2)}) copy-start(bf16[8,3584]{1,0:T(8,128)(2,1)} %param.10) | copy-start | bytes 172036
  11.1 11.2 %collective-permute-start = (bf16[6,3584]{1,0:T(8,128)(2,1)S(1)}, bf16[6,3584]{1,0:T(8,128)(2,1)S(1)}, u32[]{:S(2)}, u32[]{:S(2)}) collective-permute-start(bf16[6,3584]{1,0:T(8,128)(2,1)S(1)} %get-tuple-element.6), channel_id=1, source_target_pairs={{0,6},{2,0},{4,2},{6,4},{1,7},{3,1},{5,3},{7,5},{8,14},{10,8},{12,... | collective-permute-start | bytes 129032 | tf_op jit(solution)/shard_map/ppermute | solution.py:14
  16.2 6.1 %collective-permute-start.1 = (bf16[6,3584]{1,0:T(8,128)(2,1)S(1)}, bf16[6,3584]{1,0:T(8,128)(2,1)S(1)}, u32[]{:S(2)}, u32[]{:S(2)}) collective-permute-start(bf16[6,3584]{1,0:T(8,128)(2,1)S(1)} %get-tuple-element.5), channel_id=1, source_target_pairs={{0,4},{2,6},{4,0},{6,2},{1,5},{3,7},{5,1},{7,3},{8,12},{10,14},{12... | collective-permute-start | bytes 129032 | tf_op jit(solution)/shard_map/ppermute | solution.py:14
  16.2 6.1 %collective-permute-start.2 = (bf16[6,3584]{1,0:T(8,128)(2,1)S(1)}, bf16[6,3584]{1,0:T(8,128)(2,1)S(1)}, u32[]{:S(2)}, u32[]{:S(2)}) collective-permute-start(bf16[6,3584]{1,0:T(8,128)(2,1)S(1)} %get-tuple-element.4), channel_id=1, source_target_pairs={{0,2},{2,4},{4,6},{6,0},{1,3},{3,5},{5,7},{7,1},{8,10},{10,12},{12... | collective-permute-start | bytes 129032 | tf_op jit(solution)/shard_map/ppermute | solution.py:14
  18.2 13.1 %all-to-all-start = ((bf16[4,6,3584]{2,1,0:T(8,128)(2,1)}), bf16[4,6,3584]{2,1,0:T(8,128)(2,1)S(1)}, u32[]{:S(2)}, u32[]{:S(2)}) async-start(bf16[4,6,3584]{2,1,0:T(8,128)(2,1)} %bitcast.5), calls=%async_computation | async-start | bytes 458752 | tf_op jit(solution)/shard_map/all_to_all | solution.py:106
  22.3 32.5 %reduce-scatter.5.cloned.1.call-start = ((), (), s32[]{:S(2)}) async-start(), calls=%async_computation.6 | async-start | bytes 516096 | tf_op jit(solution)/shard_map/reduce_scatter | solution.py:56
  31.4 6.7 %copy-start.1 = (bf16[1,1,3584,256]{3,2,1,0:T(8,128)(2,1)S(1)}, bf16[1,1,3584,256]{3,2,1,0:T(8,128)(2,1)}, u32[]{:S(2)}) copy-start(bf16[1,1,3584,256]{3,2,1,0:T(8,128)(2,1)} %param.16) | copy-start | bytes 5505028
  40.5 21.1 %copy-start.4 = (bf16[8,1]{0,1:T(2,128)(2,1)S(1)}, bf16[8,1]{0,1:T(2,128)(2,1)}, u32[]{:S(2)}) copy-start(bf16[8,1]{0,1:T(2,128)(2,1)} %param.13) | copy-start | bytes 52
  40.6 29.0 %reduce-scatter.3.cloned.1.call-start = ((), (), s32[]{:S(2)}) async-start(), calls=%async_computation.5 | async-start | bytes 516096 | tf_op jit(solution)/shard_map/reduce_scatter | solution.py:53
  43.3 32.7 %copy-start.2 = (bf16[8,3584]{1,0:T(8,128)(2,1)S(1)}, bf16[8,3584]{1,0:T(8,128)(2,1)}, u32[]{:S(2)}) copy-start(bf16[8,3584]{1,0:T(8,128)(2,1)} %param.11) | copy-start | bytes 172036
  56.4 14.9 %all-to-all-start.2 = ((bf16[4,6,3584]{2,1,0:T(8,128)(2,1)}), bf16[4,6,3584]{2,1,0:T(8,128)(2,1)S(1)}, u32[]{:S(2)}, u32[]{:S(2)}) async-start(bf16[4,6,3584]{2,1,0:T(8,128)(2,1)} %all_to_all.25), calls=%async_computation.4 | async-start | bytes 458752 | tf_op jit(solution)/shard_map/all_to_all | solution.py:112
  71.3 12.8 %all-to-all-start.1 = ((bf16[4,6,3584]{2,1,0:T(8,128)(2,1)}), bf16[4,6,3584]{2,1,0:T(8,128)(2,1)S(1)}, u32[]{:S(2)}, u32[]{:S(2)}) async-start(bf16[4,6,3584]{2,1,0:T(8,128)(2,1)} %all_to_all.23), calls=%async_computation.2 | async-start | bytes 458752 | tf_op jit(solution)/shard_map/all_to_all | solution.py:111
  76.1 8.8 %collective-permute-start.3 = (bf16[8,3584]{1,0:T(8,128)(2,1)S(1)}, bf16[8,3584]{1,0:T(8,128)(2,1)S(1)}, u32[]{:S(2)}, u32[]{:S(2)}) collective-permute-start(bf16[8,3584]{1,0:T(8,128)(2,1)S(1)} %fusion.4), channel_id=1, source_target_pairs={{8,0},{16,8},{24,16},{9,1},{17,9},{25,17},{10,2},{18,10},{26,18},{... | collective-permute-start | bytes 172040 | tf_op jit(solution)/shard_map/ppermute | solution.py:22
Sparse Core Ops, SparseCore 0:
  40.7 14.0 reduce-scatter.4
  57.0 12.5 reduce-scatter.2
